TPU v7x, 32 devices: a whole 2x2x4 slice. The times are simulated.
32 devices in a mesh: band: 4 (over z), lev: 4 (over y, core), grp: 2 (over x).
Axes of the slice: x: 2, y: 2, z: 4, core: 2. Of those that a mesh axis runs over, the one named last changes fastest.
Arguments:
- fourier: bfloat16 [3, 8, 2, 2, 2, 48, 96], P(None, 'lev', None, None, 'grp', 'band'), may hold values from -6 to 6
- legendre: bfloat16 [96, 2, 48, 2, 48], P('band', None, 'lev', 'grp'), may hold values from -0.625 to 0.625
- lat_points: int32 [2, 48], P('grp', 'band'), may hold values from 20 to 400, as said below
- wave_slots: int32 [96], replicated, may hold values from 0 to 95, as said below
- vertical: float32 [8, 8], replicated, may hold values from -2 to 2
Outputs:
- spectral: bfloat16 [96, 2, 4, 8, 2, 48], P('band', None, None, None, None, ('lev', 'grp'))
Inputs may be any that keep to these rules, and one draw needn't show every extreme that they name: `lat_points`: the values are 20 + 4 i for i = 0 .. 95, each once (octahedral point counts of the latitude pairs, spread over devices). `wave_slots`: every wavenumber appears once; slots 2 i and 2 i + 1 hold wavenumbers m and 95 - m.
All inputs are finite; a program needn't handle non-finite values.
Results may differ from a plain program's by a relative error of at most 0.0053.
Values may be sent and summed in bfloat16 or wider, within the bound.
No kernel may reach another device: no remote copies, remote signals or barrier semaphores. Data moves between devices by JAX's collectives and lax.ppermute only.
A program may use at most 64 MiB of HBM per device.

v0:
```python
import jax
import jax.numpy as jnp
from jax import lax
from jax.sharding import PartitionSpec as P


def body(fourier, legendre, lat_points, wave_slots, vertical):
    wave_count = fourier.shape[6]
    cutoff = jnp.minimum(wave_count - 1, (lat_points - 1) // 2)
    wave_ids = lax.broadcasted_iota(jnp.int32, (1, 1, wave_count), 2)
    kept_mask = wave_ids <= cutoff[:, :, None]
    masked = jnp.where(kept_mask, fourier, jnp.zeros((), fourier.dtype))
    slot_table = (
        wave_slots[:, None] == lax.broadcasted_iota(jnp.int32, (wave_count, wave_count), 1)
    ).astype(jnp.bfloat16)
    ordered = lax.dot_general(
        slot_table, masked, (((1,), (6,)), ((), ())), preferred_element_type=jnp.float32
    ).astype(jnp.bfloat16)
    at_owners = lax.all_to_all(ordered, "band", split_axis=0, concat_axis=6, tiled=True)
    coeffs = lax.all_gather(at_owners, "lev", axis=2, tiled=True)
    level_count = coeffs.shape[2]
    level_rows = lax.broadcasted_iota(jnp.int32, (level_count, level_count), 0)
    level_cols = lax.broadcasted_iota(jnp.int32, (level_count, level_count), 1)
    integral = jnp.where(level_cols >= level_rows, vertical, jnp.zeros((), vertical.dtype))
    geopotential = jnp.einsum(
        "lk,skchgr->slchgr",
        integral,
        coeffs[:, 2].astype(jnp.float32),
        precision=lax.Precision.HIGHEST,
    ).astype(jnp.bfloat16)
    fields = jnp.concatenate([coeffs, geopotential[:, None]], axis=1)
    northern = fields[:, :, :, :, 0].astype(jnp.float32)
    southern = fields[:, :, :, :, 1].astype(jnp.float32)
    parity = jnp.stack(
        [(northern + southern).astype(jnp.bfloat16), (northern - southern).astype(jnp.bfloat16)],
        axis=4,
    )
    partial_value = lax.dot_general(
        parity, legendre, (((5, 6), (3, 4)), ((0, 4), (0, 1))), preferred_element_type=jnp.float32
    )
    summed = lax.psum_scatter(partial_value, "grp", scatter_dimension=5, tiled=True)
    slot_count = summed.shape[0]
    half_count = summed.shape[5]
    slot_waves = lax.dynamic_slice_in_dim(
        wave_slots, lax.axis_index("band") * slot_count, slot_count
    )
    block_start = (
        lax.axis_index("lev") * lax.axis_size("grp") + lax.axis_index("grp")
    ) * half_count
    half_ids = block_start + lax.broadcasted_iota(jnp.int32, (1, 1, half_count), 2)
    parity_ids = lax.broadcasted_iota(jnp.int32, (1, 2, 1), 1)
    total = slot_waves[:, None, None] + 2 * half_ids + parity_ids
    valid = (total <= wave_count - 1)[:, :, None, None, None, :]
    return jnp.where(valid, summed, 0.0).astype(jnp.bfloat16)


def solution(mesh):
    placed = (
        P(None, "lev", None, None, "grp", "band", None),
        P("band", None, "lev", "grp", None),
        P("grp", "band"),
        P(),
        P(),
    )
    return jax.shard_map(
        body,
        mesh=mesh,
        in_specs=placed,
        out_specs=P("band", None, None, None, None, ("lev", "grp")),
        check_vma=False,
    )
```

profile of v0, /device:TPU:0, one launch (start us, length us, event | category | flops | bytes accessed | tf_op | source)
XLA Modules:
  0.0 61.3 jit_solution(10844568631659761171)
XLA Ops:
  6.5 0.0 copy-start
  6.5 0.0 copy-start.2
  6.5 0.7 %minimum_bitcast_fusion = s32[12]{0:T(128)S(1)} fusion(s32[1,12]{1,0:T(1,128)} %param.7), kind=kLoop, calls=%fused_computation.34 | loop fusion | flops 204 | bytes 96 | tf_op jit(solution)/shard_map/le | solution.py:11
  7.3 0.1 iota_compare_fusion.1
  7.3 1.0 %fusion.9 = bf16[3,2,2,2,12,96]{5,3,4,2,1,0:T(2,128)(2,1)S(1)} fusion(bf16[3,2,2,2,1,12,96]{6,3,5,4,2,1,0:T(2,128)(2,1)} %param.5, pred[12,96]{1,0:T(8,128)(4,1)S(1)} %iota_compare_fusion.1), kind=kLoop, calls=%fused_computation.19 | loop fusion | flops 27648 | bytes 111744 | tf_op jit(solution)/shard_map/reshape.5
  8.3 0.9 %fusion.1 = bf16[96,3,2,2,2,1,12]{0,6,4,3,2,1,5:T(8,128)(2,1)S(1)} fusion(bf16[3,2,2,2,12,96]{5,3,4,2,1,0:T(2,128)(2,1)S(1)} %fusion.9, s32[96]{0:T(128)} %param.8), kind=kOutput, calls=%fused_computation.3 | convolution fusion | flops 5345280 | bytes 110976 | tf_op jit(solution)/shard_map/dot_general | solution.py:16
  9.2 0.7 %copy.19 = bf16[96,3,2,2,2,1,12]{6,4,3,2,1,5,0:T(2,128)(2,1)S(1)} copy(bf16[96,3,2,2,2,1,12]{0,6,4,3,2,1,5:T(8,128)(2,1)S(1)} %fusion.1) | data formatting | bytes 110592 | tf_op jit(solution)/shard_map/convert_element_type | solution.py:18
  9.8 1.7 %reshape.95 = bf16[4,2,3456]{2,1,0:T(2,128)(2,1)} reshape(bf16[96,1,3,2,2,2,12]{6,5,4,3,2,1,0:T(2,128)(2,1)S(1)} %bitcast.37) | data formatting | bytes 110592
  11.5 6.3 %all-to-all-start = ((bf16[4,2,3456]{2,1,0:T(2,128)(2,1)}), bf16[4,2,3456]{2,1,0:T(2,128)(2,1)S(1)}, u32[]{:S(2)}, u32[]{:S(2)}) async-start(bf16[4,2,3456]{2,1,0:T(2,128)(2,1)} %reshape.95), calls=%async_computation | async-start | bytes 110592 | tf_op jit(solution)/shard_map/all_to_all | solution.py:19
  17.9 0.0 reduce-scatter.2.cloned.1.call-start
  17.9 0.0 copy-done.2
  17.9 0.1 dynamic_slice.3
  17.9 5.6 %all-to-all-done = bf16[4,2,3456]{2,1,0:T(2,128)(2,1)S(1)} async-done(((bf16[4,2,3456]{2,1,0:T(2,128)(2,1)}), bf16[4,2,3456]{2,1,0:T(2,128)(2,1)S(1)}, u32[]{:S(2)}, u32[]{:S(2)}) %all-to-all-start) | async-done | bytes 55328 | tf_op jit(solution)/shard_map/all_to_all | solution.py:19
  23.6 1.4 %reshape.96 = bf16[96,1,3,2,2,2,12]{6,5,4,3,2,1,0:T(2,128)(2,1)S(1)} reshape(bf16[4,2,3456]{2,1,0:T(2,128)(2,1)S(1)} %all-to-all-done) | data formatting | bytes 110592
  25.0 1.0 %copy.32 = bf16[4,24,3,2,2,2,1,12]{1,0,5,7,4,3,2,6:T(4,128)(2,1)S(1)} copy(bf16[4,24,3,2,2,2,1,12]{7,5,4,3,2,1,0,6:T(2,128)(2,1)S(1)} %bitcast.38) | data formatting | bytes 110592 | tf_op jit(solution)/shard_map/all_to_all | solution.py:19
  26.0 0.0 copy-start.1
  26.0 0.2 copy.21
  26.2 0.2 copy.22
  26.4 7.6 %all_gather.3 = bf16[24,3,8,2,2,1,48]{6,0,5,4,3,1,2:T(8,128)(2,1)S(1)} all-gather(bf16[24,3,2,2,2,1,48]{6,0,5,4,3,1,2:T(8,128)(2,1)S(1)} %copy.22), channel_id=1, replica_groups=mesh['band'=4,'lev'=4,'grp'=2] {'lev'}, dimensions={2}, use_global_device_ids=true | all-gather | bytes 276480 | tf_op jit(solution)/shard_map/all_gather | solution.py:20
  34.0 0.2 copy_dynamic-update-slice_fusion
  34.2 0.0 copy-done.1
  34.2 0.3 fusion
  34.6 0.2 fusion.2
  34.8 0.0 copy-done
  34.8 0.4 fusion.4
  35.2 2.1 %copy.27 = f32[24,2,4,8,2,12]{0,3,4,2,1,5:T(8,128)} copy(f32[24,2,4,8,2,12]{5,3,4,2,1,0:T(8,128)S(1)} %fusion.4) | data formatting | bytes 294912 | tf_op jit(solution)/shard_map/dot_general | solution.py:38
  37.3 0.0 reduce-scatter.2.cloned.1.call-update
  37.3 0.1 broadcast_add_fusion
  37.4 15.2 %reduce-scatter.2.cloned.1.call-done = f32[24,2,4,8,2,6]{0,3,4,2,1,5:T(8,128)} async-done(((f32[24,2,4,8,2,12]{0,3,4,2,1,5:T(8,128)}), f32[24,2,4,8,2,6]{0,3,4,2,1,5:T(8,128)}) %reduce-scatter.2.cloned.1.call-update) | async-done | bytes 73744 | tf_op jit(solution)/shard_map/reduce_scatter | solution.py:41
  52.6 1.0 %select_convert_fusion = bf16[24,2,4,8,2,6]{0,3,4,2,1,5:T(8,128)(2,1)S(1)} fusion(f32[24,2,4,8,2,6]{0,3,4,2,1,5:T(8,128)} %reduce-scatter.2.cloned.1.call-done, pred[24,2,6]{0,1,2:T(4,128)(4,1)S(1)} %add_compare_fusion), kind=kLoop, calls=%fused_computation.13 | loop fusion | flops 18432 | bytes 110880 | tf_op jit(solution)/shard_map/convert_element_type | solution.py:54
  53.6 0.8 %copy.28 = bf16[24,2,4,8,2,6]{0,4,5,3,2,1:T(2,128)(2,1)} copy(bf16[24,2,4,8,2,6]{0,3,4,2,1,5:T(8,128)(2,1)S(1)} %select_convert_fusion) | data formatting | bytes 73728 | tf_op jit(solution)/shard_map/convert_element_type | solution.py:54
  (4 shorter events, 0.1 us)
Async XLA Ops:
  6.5 28.3 %copy-start = (bf16[24,2,12,1,48]{4,1,3,2,0:T(2,128)(2,1)S(1)}, bf16[24,2,12,1,48]{4,1,3,2,0:T(2,128)(2,1)}, u32[]{:S(2)}) copy-start(bf16[24,2,12,1,48]{4,1,3,2,0:T(2,128)(2,1)} %param.6) | copy-start | bytes 165892
  6.5 11.3 %copy-start.2 = (s32[96]{0:T(128)S(1)}, s32[96]{0:T(128)}, u32[]{:S(2)}) copy-start(s32[96]{0:T(128)} %param.8) | copy-start | bytes 1156
  11.5 12.1 %all-to-all-start = ((bf16[4,2,3456]{2,1,0:T(2,128)(2,1)}), bf16[4,2,3456]{2,1,0:T(2,128)(2,1)S(1)}, u32[]{:S(2)}, u32[]{:S(2)}) async-start(bf16[4,2,3456]{2,1,0:T(2,128)(2,1)} %reshape.95), calls=%async_computation | async-start | bytes 110592 | tf_op jit(solution)/shard_map/all_to_all | solution.py:19
  17.9 34.7 %reduce-scatter.2.cloned.1.call-start = ((), (), s32[]{:S(2)}) async-start(), calls=%async_computation.2 | async-start | bytes 1179648 | tf_op jit(solution)/shard_map/reduce_scatter | solution.py:41
  26.0 8.2 %copy-start.1 = (f32[8,8]{1,0:T(8,128)S(1)}, f32[8,8]{1,0:T(8,128)}, u32[]{:S(2)}) copy-start(f32[8,8]{1,0:T(8,128)} %param.9) | copy-start | bytes 772
Sparse Core Ops, SparseCore 0:
  37.4 15.1 reduce-scatter.1
where the time goes:
time: 61.6 us; the launch traced here: 61.3 us
  waiting for transfers between devices  20.9 us (34%)
  between operations  13.5 us (22%)
  local copies, waits for them, and re-layouts  8.37 us (14%)
  blocking collectives  7.56 us (12%)
  starting transfers between devices  6.35 us (10%)
  other arithmetic  3.09 us (5%)
  matrix products  1.56 us (3%)
    reduce_scatter x1, waiting for transfers between devices, body(): lax.psum_scatter(partial_value, 'grp', scatter_dimension=5, tiled=True)  15.2 us
    all_gather x1, blocking collectives, body(): coeffs = lax.all_gather(at_owners, 'lev', axis=2, tiled=True)  7.56 us
    all_to_all x1, starting transfers between devices, body(): lax.all_to_all(ordered, 'band', split_axis=0, concat_axis=6, tiled=True)  6.35 us
    all_to_all x1, waiting for transfers between devices, body(): lax.all_to_all(ordered, 'band', split_axis=0, concat_axis=6, tiled=True)  5.63 us
    unnamed x9, local copies, waits for them, and re-layouts  3.28 us
    dot_general x1, local copies, waits for them, and re-layouts, body(): lax.dot_general(parity, legendre, (((5, 6), (3, 4)), ((0, 4), (0, 1))), p...  2.07 us
    all_to_all x3, local copies, waits for them, and re-layouts, body(): lax.all_to_all(ordered, 'band', split_axis=0, concat_axis=6, tiled=True)  1.41 us
  transfers between devices with their start and end apart: 2, of which 2 were waited for; matrix products, arithmetic and copies ran while one was open for 0% of the time, Pallas kernels for 0%

commit v1 on v0

--- a/solution.py
+++ b/solution.py
@@ -16,7 +16,21 @@
     ordered = lax.dot_general(
         slot_table, masked, (((1,), (6,)), ((), ())), preferred_element_type=jnp.float32
     ).astype(jnp.bfloat16)
-    at_owners = lax.all_to_all(ordered, "band", split_axis=0, concat_axis=6, tiled=True)
+    arr_out = jax.lax.axis_size("band")
+    reply, earlier = (arr_out, jax.lax.axis_index("band"))
+    val = ordered.shape[0] // reply
+    mid_arr = list(ordered.shape)
+    mid_arr[0] = val
+    block_next = mid_arr[6]
+    mid_arr[6] = block_next * reply
+    at_owners = jnp.zeros(mid_arr, ordered.dtype)
+    for idx in range(reply):
+        outer = lax.dynamic_slice_in_dim(ordered, (earlier ^ idx) * val, val, axis=0)
+        if idx:
+            outer = jax.lax.ppermute(outer, "band", [(k, k ^ idx) for k in range(reply)])
+        at_owners = lax.dynamic_update_slice_in_dim(
+            at_owners, outer, (earlier ^ idx) * block_next, axis=6
+        )
     coeffs = lax.all_gather(at_owners, "lev", axis=2, tiled=True)
     level_count = coeffs.shape[2]
     level_rows = lax.broadcasted_iota(jnp.int32, (level_count, level_count), 0)

time: 61.6 us -> 67.2 us (1.091)
  local copies, waits for them, and re-layouts: 8.37 us -> 17.1 us
  waiting for transfers between devices: 20.9 us -> 18 us
    dynamic_update_slice x0 -> x4, local copies, waits for them, and re-layouts: none -> 12.5 us  [body(): lax.dynamic_update_slice_in_dim(at_owners, outer, (earlier ^ idx) * block...]
    all_to_all x1 -> x0, starting transfers between devices: 6.35 us -> none  [body(): lax.all_to_all(ordered, 'band', split_axis=0, concat_axis=6, tiled=True)]
    ppermute x0 -> x3, starting transfers between devices: none -> 5.84 us  [body(): jax.lax.ppermute(outer, 'band', [(k, k ^ idx) for k in range(reply)])]
    all_to_all x1 -> x0, waiting for transfers between devices: 5.63 us -> none  [body(): lax.all_to_all(ordered, 'band', split_axis=0, concat_axis=6, tiled=True)]
    unnamed x9 -> x7, local copies, waits for them, and re-layouts: 3.28 us -> 0.24 us
    reduce_scatter x1, waiting for transfers between devices: 15.2 us -> 17.9 us  [body(): lax.psum_scatter(partial_value, 'grp', scatter_dimension=5, tiled=True)]
    all_to_all x3 -> x0, local copies, waits for them, and re-layouts: 1.41 us -> none  [body(): lax.all_to_all(ordered, 'band', split_axis=0, concat_axis=6, tiled=True)]
    ppermute x0 -> x3, local copies, waits for them, and re-layouts: none -> 0.73 us  [body(): jax.lax.ppermute(outer, 'band', [(k, k ^ idx) for k in range(reply)])]
  transfers between devices with their start and end apart: 2 -> 4, of which waited for: 2 -> 1; matrix products, arithmetic and copies ran while one was open for 0% -> 14% of each run, Pallas kernels for 0% -> 0%
where the time goes in v1:
time: 67.2 us; the launch traced here: 66.9 us
  waiting for transfers between devices  18 us (27%)
  local copies, waits for them, and re-layouts  17.1 us (25%)
  between operations  13.6 us (20%)
  blocking collectives  7.72 us (11%)
  starting transfers between devices  5.84 us (9%)
  other arithmetic  3.09 us (5%)
  matrix products  1.56 us (2%)
    reduce_scatter x1, waiting for transfers between devices, body(): lax.psum_scatter(partial_value, 'grp', scatter_dimension=5, tiled=True)  17.9 us
    dynamic_update_slice x4, local copies, waits for them, and re-layouts, body(): lax.dynamic_update_slice_in_dim(at_owners, outer, (earlier ^ idx) * block...  12.5 us
    all_gather x1, blocking collectives, body(): coeffs = lax.all_gather(at_owners, 'lev', axis=2, tiled=True)  7.72 us
    ppermute x3, starting transfers between devices, body(): jax.lax.ppermute(outer, 'band', [(k, k ^ idx) for k in range(reply)])  5.84 us
    dot_general x1, local copies, waits for them, and re-layouts, body(): lax.dot_general(parity, legendre, (((5, 6), (3, 4)), ((0, 4), (0, 1))), p...  2.06 us
  transfers between devices with their start and end apart: 4, of which 1 were waited for; matrix products, arithmetic and copies ran while one was open for 14% of the time, Pallas kernels for 0%

profile of v1, /device:TPU:0, one launch (start us, length us, event | category | flops | bytes accessed | tf_op | source)
XLA Modules:
  0.0 66.9 jit_solution(3072772737461175576)
XLA Ops:
  6.5 0.0 copy-start
  6.5 0.0 copy-start.2
  6.5 0.0 reduce-scatter.2.cloned.1.call-start
  6.5 0.7 %minimum_bitcast_fusion = s32[12]{0:T(128)S(1)} fusion(s32[1,12]{1,0:T(1,128)} %param.7), kind=kLoop, calls=%fused_computation.40 | loop fusion | flops 204 | bytes 96 | tf_op jit(solution)/shard_map/le | solution.py:11
  7.3 0.1 iota_compare_fusion.1
  7.3 1.0 %fusion.8 = bf16[3,2,2,2,12,96]{5,3,4,2,1,0:T(2,128)(2,1)S(1)} fusion(bf16[3,2,2,2,1,12,96]{6,3,5,4,2,1,0:T(2,128)(2,1)} %param.5, pred[12,96]{1,0:T(8,128)(4,1)S(1)} %iota_compare_fusion.1), kind=kLoop, calls=%fused_computation.19 | loop fusion | flops 27648 | bytes 111744 | tf_op jit(solution)/shard_map/reshape.5
  8.3 0.9 %convolution_convert_fusion.1 = bf16[96,3,2,2,2,12]{0,5,4,3,2,1:T(8,128)(2,1)S(1)} fusion(bf16[3,2,2,2,12,96]{5,3,4,2,1,0:T(2,128)(2,1)S(1)} %fusion.8, s32[96]{0:T(128)} %param.8), kind=kOutput, calls=%fused_computation.2 | convolution fusion | flops 5345280 | bytes 110976 | tf_op jit(solution)/shard_map/dot_general | solution.py:16
  9.2 0.2 constant_dynamic-slice_fusion
  9.4 0.1 copy.58
  9.4 3.1 %collective-permute-start = (bf16[24,3,2,2,2,1,12]{0,4,6,3,2,1,5:T(2,128)(2,1)S(1)}, bf16[24,3,2,2,2,1,12]{0,4,6,3,2,1,5:T(2,128)(2,1)S(1)}, u32[]{:S(2)}, u32[]{:S(2)}) collective-permute-start(bf16[24,3,2,2,2,1,12]{0,4,6,3,2,1,5:T(2,128)(2,1)S(1)} %bitcast.43), channel_id=1, source_target_pairs={{0,8},{8,0},{16,24},{24,16},{1,9},{9,1},{17,25},{25,17},{2,10},{10... | collective-permute-start | bytes 41480 | tf_op jit(solution)/shard_map/ppermute | solution.py:30
  12.6 0.1 copy.57
  12.6 2.7 %collective-permute-start.1 = (bf16[24,3,2,2,2,1,12]{0,4,6,3,2,1,5:T(2,128)(2,1)S(1)}, bf16[24,3,2,2,2,1,12]{0,4,6,3,2,1,5:T(2,128)(2,1)S(1)}, u32[]{:S(2)}, u32[]{:S(2)}) collective-permute-start(bf16[24,3,2,2,2,1,12]{0,4,6,3,2,1,5:T(2,128)(2,1)S(1)} %bitcast.42), channel_id=1, source_target_pairs={{0,16},{8,24},{16,0},{24,8},{1,17},{9,25},{17,1},{25,9},{2,18},{10... | collective-permute-start | bytes 41480 | tf_op jit(solution)/shard_map/ppermute | solution.py:30
  15.3 0.1 copy.56
  15.3 0.1 collective-permute-start.2
  15.5 0.0 copy-done.2
  15.5 0.1 dynamic_slice.15
  15.5 0.2 copy.24
  15.8 0.6 dynamic_update_slice.12
  16.5 0.0 collective-permute-done
  16.5 0.2 copy.26
  16.7 4.0 %dynamic_update_slice.13 = bf16[24,3,2,2,2,1,48]{6,0,5,4,3,1,2:T(8,128)(2,1)S(1)} dynamic-update-slice(bf16[24,3,2,2,2,1,48]{6,0,5,4,3,1,2:T(8,128)(2,1)S(1)} %dynamic_update_slice.12, bf16[24,3,2,2,2,1,12]{6,0,5,4,3,1,2:T(8,128)(2,1)S(1)} %copy.26, s32[]{:T(128)} %constant.17.clone.1, s32[]{:T(128)} %constant.17.clone.1, s32[]{:T(128)} %constant.17.clone.1, s32[]{:T(128)} %constant.17.clone.1, ...) | dynamic-update-slice | bytes 27652 | tf_op jit(solution)/shard_map/dynamic_update_slice | solution.py:31
  20.7 0.0 collective-permute-done.1
  20.7 0.2 copy.28
  20.9 0.0 copy-start.1
  20.9 4.0 %dynamic_update_slice.14 = bf16[24,3,2,2,2,1,48]{6,0,5,4,3,1,2:T(8,128)(2,1)S(1)} dynamic-update-slice(bf16[24,3,2,2,2,1,48]{6,0,5,4,3,1,2:T(8,128)(2,1)S(1)} %dynamic_update_slice.13, bf16[24,3,2,2,2,1,12]{6,0,5,4,3,1,2:T(8,128)(2,1)S(1)} %copy.28, s32[]{:T(128)} %constant.17.clone.1, s32[]{:T(128)} %constant.17.clone.1, s32[]{:T(128)} %constant.17.clone.1, s32[]{:T(128)} %constant.17.clone.1, ...) | dynamic-update-slice | bytes 27652 | tf_op jit(solution)/shard_map/dynamic_update_slice | solution.py:31
  24.9 0.0 collective-permute-done.2
  24.9 0.2 copy.30
  25.2 4.0 %dynamic_update_slice.15 = bf16[24,3,2,2,2,1,48]{6,0,5,4,3,1,2:T(8,128)(2,1)S(1)} dynamic-update-slice(bf16[24,3,2,2,2,1,48]{6,0,5,4,3,1,2:T(8,128)(2,1)S(1)} %dynamic_update_slice.14, bf16[24,3,2,2,2,1,12]{6,0,5,4,3,1,2:T(8,128)(2,1)S(1)} %copy.30, s32[]{:T(128)} %constant.17.clone.1, s32[]{:T(128)} %constant.17.clone.1, s32[]{:T(128)} %constant.17.clone.1, s32[]{:T(128)} %constant.17.clone.1, ...) | dynamic-update-slice | bytes 27652 | tf_op jit(solution)/shard_map/dynamic_update_slice | solution.py:31
  29.1 7.7 %all_gather.3 = bf16[24,3,8,2,2,1,48]{6,0,5,4,3,1,2:T(8,128)(2,1)S(1)} all-gather(bf16[24,3,2,2,2,1,48]{6,0,5,4,3,1,2:T(8,128)(2,1)S(1)} %dynamic_update_slice.15), channel_id=1, replica_groups=mesh['band'=4,'lev'=4,'grp'=2] {'lev'}, dimensions={2}, use_global_device_ids=true | all-gather | bytes 276480 | tf_op jit(solution)/shard_map/all_gather | solution.py:34
  36.9 0.2 copy_dynamic-update-slice_fusion
  37.1 0.0 copy-done.1
  37.1 0.3 fusion
  37.5 0.2 fusion.1
  37.7 0.0 copy-done
  37.7 0.4 fusion.3
  38.1 2.1 %copy.35 = f32[24,2,4,8,2,12]{0,3,4,2,1,5:T(8,128)} copy(f32[24,2,4,8,2,12]{5,3,4,2,1,0:T(8,128)S(1)} %fusion.3) | data formatting | bytes 294912 | tf_op jit(solution)/shard_map/dot_general | solution.py:52
  40.2 0.0 reduce-scatter.2.cloned.1.call-update
  40.2 0.1 broadcast_add_fusion
  40.3 17.9 %reduce-scatter.2.cloned.1.call-done = f32[24,2,4,8,2,6]{0,3,4,2,1,5:T(8,128)} async-done(((f32[24,2,4,8,2,12]{0,3,4,2,1,5:T(8,128)}), f32[24,2,4,8,2,6]{0,3,4,2,1,5:T(8,128)}) %reduce-scatter.2.cloned.1.call-update) | async-done | bytes 73744 | tf_op jit(solution)/shard_map/reduce_scatter | solution.py:55
  58.2 1.0 %select_convert_fusion = bf16[24,2,4,8,2,6]{0,3,4,2,1,5:T(8,128)(2,1)S(1)} fusion(f32[24,2,4,8,2,6]{0,3,4,2,1,5:T(8,128)} %reduce-scatter.2.cloned.1.call-done, pred[24,2,6]{0,1,2:T(4,128)(4,1)S(1)} %add_compare_fusion), kind=kLoop, calls=%fused_computation.12 | loop fusion | flops 18432 | bytes 110880 | tf_op jit(solution)/shard_map/convert_element_type | solution.py:68
  59.3 0.8 %copy.36 = bf16[24,2,4,8,2,6]{0,4,5,3,2,1:T(2,128)(2,1)} copy(bf16[24,2,4,8,2,6]{0,3,4,2,1,5:T(8,128)(2,1)S(1)} %select_convert_fusion) | data formatting | bytes 73728 | tf_op jit(solution)/shard_map/convert_element_type | solution.py:68
  (5 shorter events, 0.1 us)
Async XLA Ops:
  6.5 31.2 %copy-start = (bf16[24,2,12,1,48]{4,1,3,2,0:T(2,128)(2,1)S(1)}, bf16[24,2,12,1,48]{4,1,3,2,0:T(2,128)(2,1)}, u32[]{:S(2)}) copy-start(bf16[24,2,12,1,48]{4,1,3,2,0:T(2,128)(2,1)} %param.6) | copy-start | bytes 165892
  6.5 8.9 %copy-start.2 = (s32[96]{0:T(128)S(1)}, s32[96]{0:T(128)}, u32[]{:S(2)}) copy-start(s32[96]{0:T(128)} %param.8) | copy-start | bytes 1156
  6.5 51.7 %reduce-scatter.2.cloned.1.call-start = ((), (), s32[]{:S(2)}) async-start(), calls=%async_computation.1 | async-start | bytes 1179648 | tf_op jit(solution)/shard_map/reduce_scatter | solution.py:55
  9.4 7.0 %collective-permute-start = (bf16[24,3,2,2,2,1,12]{0,4,6,3,2,1,5:T(2,128)(2,1)S(1)}, bf16[24,3,2,2,2,1,12]{0,4,6,3,2,1,5:T(2,128)(2,1)S(1)}, u32[]{:S(2)}, u32[]{:S(2)}) collective-permute-start(bf16[24,3,2,2,2,1,12]{0,4,6,3,2,1,5:T(2,128)(2,1)S(1)} %bitcast.43), channel_id=1, source_target_pairs={{0,8},{8,0},{16,24},{24,16},{1,9},{9,1},{17,25},{25,17},{2,10},{10... | collective-permute-start | bytes 41480 | tf_op jit(solution)/shard_map/ppermute | solution.py:30
  12.6 8.1 %collective-permute-start.1 = (bf16[24,3,2,2,2,1,12]{0,4,6,3,2,1,5:T(2,128)(2,1)S(1)}, bf16[24,3,2,2,2,1,12]{0,4,6,3,2,1,5:T(2,128)(2,1)S(1)}, u32[]{:S(2)}, u32[]{:S(2)}) collective-permute-start(bf16[24,3,2,2,2,1,12]{0,4,6,3,2,1,5:T(2,128)(2,1)S(1)} %bitcast.42), channel_id=1, source_target_pairs={{0,16},{8,24},{16,0},{24,8},{1,17},{9,25},{17,1},{25,9},{2,18},{10... | collective-permute-start | bytes 41480 | tf_op jit(solution)/shard_map/ppermute | solution.py:30
  15.3 9.6 %collective-permute-start.2 = (bf16[24,3,2,2,2,1,12]{0,4,6,3,2,1,5:T(2,128)(2,1)S(1)}, bf16[24,3,2,2,2,1,12]{0,4,6,3,2,1,5:T(2,128)(2,1)S(1)}, u32[]{:S(2)}, u32[]{:S(2)}) collective-permute-start(bf16[24,3,2,2,2,1,12]{0,4,6,3,2,1,5:T(2,128)(2,1)S(1)} %bitcast.41), channel_id=1, source_target_pairs={{0,24},{8,16},{16,8},{24,0},{1,25},{9,17},{17,9},{25,1},{2,26},{10... | collective-permute-start | bytes 41480 | tf_op jit(solution)/shard_map/ppermute | solution.py:30
  20.9 16.2 %copy-start.1 = (f32[8,8]{1,0:T(8,128)S(1)}, f32[8,8]{1,0:T(8,128)}, u32[]{:S(2)}) copy-start(f32[8,8]{1,0:T(8,128)} %param.9) | copy-start | bytes 772
Sparse Core Ops, SparseCore 0:
  40.3 17.8 reduce-scatter.1
